TPU v7x, 32 devices: a whole 2x2x4 slice. The times are simulated.
32 devices in a mesh: ctx: 8 (over y, x, core), chan: 4 (over z).
Axes of the slice: x: 2, y: 2, z: 4, core: 2. Of those that a mesh axis runs over, the one named last changes fastest.
Arguments:
- value_branch: bfloat16 [192, 65536], P(None, ('ctx', 'chan')), may hold values from -6 to 6
- key_branch: bfloat16 [192, 65536], P(None, ('ctx', 'chan')), may hold values from -6 to 6
- gate_branch: bfloat16 [192, 65536], P(None, ('ctx', 'chan')), may hold values from -6 to 6
- skip_gain: float32 [192], replicated, may hold values from -4 to 4
- spectra: float32 [2, 192, 8, 8192], P(None, 'chan', 'ctx'), may hold values from -6 to 6
Outputs:
- gated_output: bfloat16 [192, 65536], P(None, ('ctx', 'chan'))
All inputs are finite; a program needn't handle non-finite values.
Results may differ from a plain program's by a relative error of at most 0.0054.
Values may be sent and summed in bfloat16 or wider, within the bound.
A program may use at most 64 MiB of HBM per device.

v0:
```python
import functools
import math

import jax
import jax.numpy as jnp
import numpy as np
from jax import lax
from jax.experimental import pallas as pl
from jax.experimental.pallas import tpu as pltpu
from jax.sharding import PartitionSpec as P

two_pi = 2.0 * math.pi
first_factor = 128
highest = lax.Precision.HIGHEST


def reversed_bits(numbers, bit_count):
    result = numbers * 0
    for bit_number in range(bit_count):
        result = result + (numbers >> bit_number & 1) * (1 << bit_count - 1 - bit_number)
    return result


def phase_pair(radians):
    return (jnp.cos(radians), jnp.sin(radians))


def block_table(length_of, direction):
    counter = jnp.arange(length_of, dtype=jnp.int32)
    product = counter[:, None] * counter[None, :] % length_of
    cosine, sine = phase_pair(direction * two_pi / length_of * product.astype(jnp.float32))
    upper_rows = jnp.stack([cosine, -sine], axis=1)
    lower_rows = jnp.stack([sine, cosine], axis=1)
    return jnp.stack([upper_rows, lower_rows], axis=0)


def complex_mul(signal, factor):
    factor_real, factor_imag = factor
    return jnp.stack(
        [
            signal[0] * factor_real - signal[1] * factor_imag,
            signal[0] * factor_imag + signal[1] * factor_real,
        ]
    )


def forward_local(signal):
    channel_count, seq_length = (signal.shape[1], signal.shape[2])
    second_factor = seq_length // first_factor
    blocked = signal.reshape(2, channel_count, first_factor, second_factor)
    section_one = jnp.einsum(
        "orca,cxaq->oxrq", block_table(first_factor, -1.0), blocked, precision=highest
    )
    column = jnp.arange(first_factor, dtype=jnp.int32)[:, None]
    within = jnp.arange(second_factor, dtype=jnp.int32)[None, :]
    twiddle = phase_pair(-two_pi / seq_length * (column * within).astype(jnp.float32))
    section_two = complex_mul(section_one, twiddle)
    section_three = jnp.einsum(
        "peoq,oxrq->pxer", block_table(second_factor, -1.0), section_two, precision=highest
    )
    return section_three.reshape(2, channel_count, seq_length)


def inverse_local(signal):
    channel_count, seq_length = (signal.shape[1], signal.shape[2])
    second_factor = seq_length // first_factor
    blocked = signal.reshape(2, channel_count, second_factor, first_factor)
    section_one = jnp.einsum(
        "pqoe,oxer->pxqr", block_table(second_factor, 1.0), blocked, precision=highest
    )
    within = jnp.arange(second_factor, dtype=jnp.int32)[:, None]
    column = jnp.arange(first_factor, dtype=jnp.int32)[None, :]
    twiddle = phase_pair(two_pi / seq_length * (within * column).astype(jnp.float32))
    section_two = complex_mul(section_one, twiddle)
    section_three = jnp.einsum(
        "paor,oxqr->pxaq", block_table(first_factor, 1.0), section_two, precision=highest
    )
    return section_three.reshape(2, channel_count, seq_length)


def blockwise_body(value_branch, key_branch, gate_branch, skip_gain, spectra):
    carried = (key_branch.astype(jnp.float32) * value_branch.astype(jnp.float32)).astype(
        jnp.bfloat16
    )
    series = lax.all_to_all(carried, "chan", split_axis=0, concat_axis=1, tiled=True)
    channel_count, seq_length = series.shape
    ctx_count = lax.axis_size("ctx")
    bit_count = ctx_count.bit_length() - 1
    device = lax.axis_index("ctx")
    total_length = seq_length * ctx_count
    counter = jnp.arange(ctx_count, dtype=jnp.int32)
    target = reversed_bits(counter, bit_count)
    blocks = lax.all_to_all(
        series.reshape(channel_count, 1, seq_length), "ctx", split_axis=2, concat_axis=1, tiled=True
    )
    matrix = jnp.stack(
        phase_pair(
            -two_pi
            / ctx_count
            * (target[:, None] * counter[None, :] % ctx_count).astype(jnp.float32)
        )
    )
    rows = jnp.einsum("ojp,xps->oxjs", matrix, blocks.astype(jnp.float32), precision=highest)
    received = lax.all_to_all(rows, "ctx", split_axis=2, concat_axis=3, tiled=True)
    signal = received.reshape(2, channel_count, seq_length)
    device_rank = reversed_bits(device, bit_count)
    positions = jnp.arange(seq_length, dtype=jnp.int32)
    radians = two_pi / total_length * (positions * device_rank).astype(jnp.float32)
    signal = complex_mul(signal, phase_pair(-radians))
    spectrum = forward_local(signal)
    shaped = complex_mul(spectrum, (spectra[0, :, 0, :], spectra[1, :, 0, :]))
    returned = complex_mul(inverse_local(shaped), phase_pair(radians))
    parts = lax.all_to_all(
        returned.reshape(2, channel_count, 1, seq_length),
        "ctx",
        split_axis=3,
        concat_axis=2,
        tiled=True,
    )
    cosine, sine = phase_pair(
        two_pi / ctx_count * (counter[:, None] * target[None, :] % ctx_count).astype(jnp.float32)
    )
    matrix = jnp.stack([cosine, -sine])
    summed = jnp.einsum("opj,oxjs->xps", matrix, parts, precision=highest) / total_length
    local_conv = summed.astype(jnp.bfloat16)
    convolved = lax.all_to_all(local_conv, "ctx", split_axis=1, concat_axis=2, tiled=True).reshape(
        channel_count, seq_length
    )
    tokens_conv = lax.all_to_all(convolved, "chan", split_axis=1, concat_axis=0, tiled=True)
    result = gate_branch.astype(jnp.float32) * (
        tokens_conv.astype(jnp.float32) + skip_gain[:, None] * carried.astype(jnp.float32)
    )
    return result.astype(jnp.bfloat16)


lanes = 128
MESH = pl.DeviceIdType.MESH
VMEM = pl.BlockSpec(memory_space=pltpu.VMEM)


@functools.lru_cache(maxsize=None)
def transform_tables(rows_total, ctx_count):
    length = rows_total * lanes
    bit_count = ctx_count.bit_length() - 1
    rev = np.array([int(format(j, "b").zfill(bit_count)[::-1], 2) if bit_count else 0 for j in range(ctx_count)])
    a = np.arange(rows_total // ctx_count)
    k1 = (rev[:, None] + ctx_count * a[None, :]).reshape(-1)
    fold = lanes // (rows_total // ctx_count)
    k2 = np.arange(lanes).reshape(lanes // fold, fold).T.reshape(-1)
    n1, n2 = np.arange(rows_total), np.arange(lanes)
    f1 = np.exp(-2j * np.pi * (np.outer(k1, n1) % rows_total) / rows_total)
    f2 = np.exp(-2j * np.pi * (np.outer(n2, k2) % lanes) / lanes)
    tw = np.exp(-2j * np.pi * (np.outer(k1, n2) % length) / length)
    w1 = np.stack([f1.real, f1.imag])
    w2 = np.block([[f2.real, f2.imag], [-f2.imag, f2.real]])
    b2 = f2.conj().T
    w3 = np.block([[b2.real, b2.imag], [-b2.imag, b2.real]])
    b1 = f1.conj().T / length
    v1 = np.concatenate([b1.real, -b1.imag], axis=1)
    half = lambda t: np.asarray(t, dtype=jnp.bfloat16)
    return half(w1), half(w2), half(w3), half(v1), np.stack([tw.real, tw.imag]).astype(np.float32)


def greet_all(ctx_count, chan_count, me):
    total = ctx_count * chan_count
    barrier = pltpu.get_barrier_semaphore()

    @pl.loop(1, total)
    def _(offset):
        other = lax.rem(me + offset, total)
        pl.semaphore_signal(
            barrier, inc=1, device_id=(other // chan_count, lax.rem(other, chan_count)), device_id_type=MESH
        )


def dot(a, b):
    return jnp.dot(a, b, preferred_element_type=jnp.float32)


def fused_kernel(ctx_count, chan_count, skip_ref, v_hbm, k_hbm, gate_hbm, s_hbm, *refs):
    tables_hbm, (out_ref,), tables = refs[:5], refs[5:6], refs[6:11]
    w1_ref, w2_ref, w3_ref, v1_ref, tw_ref = tables
    s_ref, stage, r_ref, x_ref, y_ref, g_ref = refs[11:17]
    v_ref, k_ref, gate_ref, c_ref, o_ref = refs[17:22]
    send_c, recv_c, send_s, recv_s, send_y, recv_y, local = refs[22:]
    ctx, chan = lax.axis_index("ctx"), lax.axis_index("chan")
    me = ctx * chan_count + chan
    total = ctx_count * chan_count
    pairs, rows = x_ref.shape[0], c_ref.shape[1]
    rows_total = x_ref.shape[1]
    block = stage.shape[2]
    local_channels = stage.shape[1]

    greet_all(ctx_count, chan_count, me)
    sources = (v_hbm, k_hbm, s_hbm, gate_hbm, *tables_hbm)
    targets = (v_ref, k_ref, s_ref, gate_ref, *tables)
    loads = [
        pltpu.make_async_copy(source, target, local.at[i]) for i, (source, target) in enumerate(zip(sources, targets))
    ]
    for load in loads:
        load.start()
    group = 2 * ctx_count
    loads[0].wait()
    loads[1].wait()

    def pack(pair):
        @pl.loop(0, chan_count)
        def _(chan_index):
            index = chan_index * pairs + pair
            at = pl.ds(pl.multiple_of(index * group, group), group)
            product = (k_ref[at].astype(jnp.float32) * v_ref[at].astype(jnp.float32)).astype(jnp.bfloat16)
            split = product.astype(jnp.float32).reshape(ctx_count, 2, rows, lanes)
            packed = jnp.concatenate([split[:, 0], split[:, 1]], axis=2)
            c_ref[pl.ds(index * ctx_count, ctx_count)] = packed.astype(jnp.bfloat16)


    def place(offset):
        other = lax.rem(me + offset, total)
        return other, other // chan_count, lax.rem(other, chan_count)

    def slot(ctx_index, chan_index, pair):
        return (chan_index * pairs + pair) * ctx_count + ctx_index

    my_rows = pl.ds(pl.multiple_of(me * rows, rows), rows)
    my_block = pl.ds(pl.multiple_of(ctx * block, block), block)

    def carried_copy(pair, offset):
        other, other_ctx, other_chan = place(offset)
        return pltpu.make_async_remote_copy(
            src_ref=c_ref.at[slot(other_ctx, other_chan, pair)],
            dst_ref=x_ref.at[pair, my_rows],
            send_sem=send_c.at[pair, offset - 1],
            recv_sem=recv_c.at[pair, offset - 1],
            device_id=(other_ctx, other_chan),
            device_id_type=MESH,
        )

    def spectra_copy(pair, offset):
        other_ctx = lax.rem(ctx + offset, ctx_count)
        return pltpu.make_async_remote_copy(
            src_ref=stage.at[:, pl.ds((pair * ctx_count + other_ctx) * 2, 2)],
            dst_ref=r_ref.at[:, pl.ds(2 * pair, 2), my_block],
            send_sem=send_s.at[pair, offset - 1],
            recv_sem=recv_s.at[pair, offset - 1],
            device_id=(other_ctx, chan),
            device_id_type=MESH,
        )

    def result_copy(pair, offset):
        other, other_ctx, other_chan = place(offset)
        return pltpu.make_async_remote_copy(
            src_ref=y_ref.at[pair, pl.ds(pl.multiple_of(other * rows, rows), rows)],
            dst_ref=o_ref.at[slot(ctx, chan, pair)],
            send_sem=send_y.at[pair, offset - 1],
            recv_sem=recv_y.at[pair, offset - 1],
            device_id=(other_ctx, other_chan),
            device_id_type=MESH,
        )

    def each(copy_of, pair, count, act):
        @pl.loop(1, count)
        def _(offset):
            act(copy_of(pair, offset))

    def turned(part, channel):
        flipped = s_ref[part * local_channels + channel].T
        pieces = [flipped[f * block : (f + 1) * block] for f in range(flipped.shape[0] // block)]
        return jnp.concatenate(pieces, axis=1).astype(jnp.bfloat16)

    def turn(pair):
        @pl.loop(1, ctx_count)
        def _(offset):
            first = (pair * ctx_count + lax.rem(ctx + offset, ctx_count)) * 2
            for part in range(2):
                for which in range(2):
                    stage[part, first + which] = turned(part, first + which)

        for part in range(2):
            for which in range(2):
                r_ref[part, 2 * pair + which, my_block] = turned(part, (pair * ctx_count + ctx) * 2 + which)
        x_ref[pair, my_rows] = c_ref[slot(ctx, chan, pair)]

    start = lambda copy: copy.start()
    pack(0)
    pl.semaphore_wait(pltpu.get_barrier_semaphore(), total - 1)
    each(carried_copy, 0, total, start)
    for pair in range(1, pairs):
        pack(pair)
        each(carried_copy, pair, total, start)
    loads[2].wait()
    for pair in range(pairs):
        turn(pair)
        each(spectra_copy, pair, ctx_count, start)
    for load in loads[3:]:
        load.wait()
    chunk = 2 * lanes
    for pair in range(pairs):
        each(carried_copy, pair, total, lambda copy: copy.wait_recv())
        each(spectra_copy, pair, ctx_count, lambda copy: copy.wait_recv())
        x = x_ref.at[pair]

        @pl.loop(0, rows_total // chunk)
        def _(step):
            at = pl.ds(pl.multiple_of(step * chunk, chunk), chunk)
            below = pl.ds(pl.multiple_of(rows_total + step * chunk, chunk), chunk)
            real, imag = dot(w1_ref[0, at], x[...]), dot(w1_ref[1, at], x[...])
            t_real, t_imag = tw_ref[0, at], tw_ref[1, at]
            for which in range(2):
                cols = slice(which * lanes, (which + 1) * lanes)
                a_real, a_imag = real[:, cols], imag[:, cols]
                twiddled = jnp.concatenate(
                    [a_real * t_real - a_imag * t_imag, a_real * t_imag + a_imag * t_real], axis=1
                )
                bins = dot(twiddled.astype(jnp.bfloat16), w2_ref[...])
                b_real, b_imag = bins[:, :lanes], bins[:, lanes:]
                f_real = r_ref[0, 2 * pair + which, at].astype(jnp.float32)
                f_imag = r_ref[1, 2 * pair + which, at].astype(jnp.float32)
                shaped = jnp.concatenate(
                    [b_real * f_real - b_imag * f_imag, b_real * f_imag + b_imag * f_real], axis=1
                )
                back = dot(shaped.astype(jnp.bfloat16), w3_ref[...])
                z_real, z_imag = back[:, :lanes], back[:, lanes:]
                g_ref[at, cols] = (z_real * t_real + z_imag * t_imag).astype(jnp.bfloat16)
                g_ref[below, cols] = (z_imag * t_real - z_real * t_imag).astype(jnp.bfloat16)

        @pl.loop(0, rows_total // chunk)
        def _(step):
            at = pl.ds(pl.multiple_of(step * chunk, chunk), chunk)
            y_ref[pair, at] = dot(v1_ref[at], g_ref[...]).astype(jnp.bfloat16)

        o_ref[slot(ctx, chan, pair)] = y_ref[pair, my_rows]
        each(result_copy, pair, total, start)

    for pair in range(pairs):
        each(result_copy, pair, total, lambda copy: copy.wait_recv())

        @pl.loop(0, chan_count)
        def _(chan_index):
            first = slot(0, chan_index, pair)
            sums = []
            for i in range(ctx_count):
                for which in range(2):
                    cols = slice(which * lanes, (which + 1) * lanes)
                    carried = c_ref[first + i, :, cols].astype(jnp.float32)
                    gain = skip_ref[2 * (first + i) + which]
                    sums.append(o_ref[first + i, :, cols].astype(jnp.float32) + gain * carried)
            flat = jnp.stack(sums).reshape(group, rows * lanes)
            at = pl.ds(pl.multiple_of(first * 2, group), group)
            out_ref[at] = (gate_ref[at].astype(jnp.float32) * flat).astype(jnp.bfloat16)

    for pair in range(pairs):
        each(carried_copy, pair, total, lambda copy: copy.wait_send())
        each(spectra_copy, pair, ctx_count, lambda copy: copy.wait_send())
        each(result_copy, pair, total, lambda copy: copy.wait_send())


def channel_body(value_branch, key_branch, gate_branch, skip_gain, spectra):
    channels, tokens = value_branch.shape
    ctx_count, chan_count = lax.axis_size("ctx"), lax.axis_size("chan")
    total = ctx_count * chan_count
    rows = tokens // lanes
    rows_total = rows * total
    pairs = channels // total // 2
    local_channels = spectra.shape[1]
    block = spectra.shape[3] // lanes
    tables = [jnp.asarray(t) for t in transform_tables(rows_total, ctx_count)]
    sems = lambda *shape: pltpu.SemaphoreType.DMA(shape)
    hbm = pl.BlockSpec(memory_space=pl.ANY)
    packed = pltpu.VMEM((channels // 2, rows, 2 * lanes), jnp.bfloat16)
    held = pltpu.VMEM((channels, tokens), jnp.bfloat16)
    return pl.pallas_call(
        functools.partial(fused_kernel, ctx_count, chan_count),
        in_specs=[pl.BlockSpec(memory_space=pltpu.SMEM)] + [hbm] * 9,
        out_specs=VMEM,
        out_shape=jax.ShapeDtypeStruct((channels, tokens), jnp.bfloat16),
        scratch_shapes=[pltpu.VMEM(t.shape, t.dtype) for t in tables]
        + [
            pltpu.VMEM((2 * local_channels, block, lanes), jnp.float32),
            pltpu.VMEM((2, local_channels, block, lanes), jnp.bfloat16),
            pltpu.VMEM((2, 2 * pairs, rows_total, lanes), jnp.bfloat16),
            pltpu.VMEM((pairs, rows_total, 2 * lanes), jnp.bfloat16),
            pltpu.VMEM((pairs, rows_total, 2 * lanes), jnp.bfloat16),
            pltpu.VMEM((2 * rows_total, 2 * lanes), jnp.bfloat16),
            held, held, held, packed, packed,
        ]
        + [sems(pairs, count - 1) for count in (total, total, ctx_count, ctx_count, total, total)]
        + [sems(9)],
        compiler_params=pltpu.CompilerParams(collective_id=0, has_side_effects=True),
    )(
        skip_gain,
        value_branch,
        key_branch,
        gate_branch,
        spectra.reshape(2 * local_channels, block, lanes),
        *tables,
    )


def body(value_branch, key_branch, gate_branch, skip_gain, spectra):
    channels, tokens = value_branch.shape
    ctx_count, chan_count = lax.axis_size("ctx"), lax.axis_size("chan")
    total = ctx_count * chan_count
    block_rows = tokens * chan_count // lanes
    fits = (
        channels % (2 * total) == 0
        and ctx_count % 8 == 0
        and tokens % (16 * lanes) == 0
        and block_rows <= lanes
        and lanes % block_rows == 0
        and (tokens * total // lanes) % lanes == 0
    )
    chosen = channel_body if fits else blockwise_body
    return chosen(value_branch, key_branch, gate_branch, skip_gain, spectra)


def solution(mesh):
    in_specs = (
        P(None, ("ctx", "chan")),
        P(None, ("ctx", "chan")),
        P(None, ("ctx", "chan")),
        P(),
        P(None, "chan", "ctx", None),
    )
    out_specs = P(None, ("ctx", "chan"))
    return jax.shard_map(body, mesh=mesh, in_specs=in_specs, out_specs=out_specs, check_vma=False)
```

profile of v0, /device:TPU:0, one launch (start us, length us, event | category | flops | bytes accessed | tf_op | source)
XLA Modules:
  0.0 55.9 jit_solution(17769067251820746361)
XLA Ops:
  0.0 53.8 %shard_map.100 = bf16[192,2048]{1,0:T(8,128)(2,1)} custom-call(f32[192]{0:T(256)} %skip_ref.1, bf16[192,2048]{1,0:T(8,128)(2,1)} %v_hbm.1, bf16[192,2048]{1,0:T(8,128)(2,1)} %k_hbm.1, bf16[192,2048]{1,0:T(8,128)(2,1)} %gate_hbm.1, f32[96,64,128]{2,1,0:T(8,128)} %bitcast.1, bf16[2,512,512]{2,1,0:T(8,128)(2,1)} %constant.10.clone.refs_0_, ...), custom_call_target="tpu_custom_call" | custom-call | tf_op jit(solution)/shard_map/pallas_call | solution.py:371
  53.8 2.1 %copy.12 = bf16[192,2048]{1,0:T(8,128)(2,1)} copy(bf16[192,2048]{1,0:T(8,128)(2,1)} %shard_map.100) | data formatting | bytes 1572864
where the time goes:
time: 56 us; the launch traced here: 55.9 us
  Pallas kernels  53.8 us (96%)
  local copies, waits for them, and re-layouts  2.09 us (4%)
    pallas_call x1, Pallas kernels, channel_body(): pl.pallas_call(functools.partial(fused_kernel, ctx_count, chan_count), in...  53.8 us
    unnamed x1, local copies, waits for them, and re-layouts  2.09 us

commit v1 on v0

--- a/solution.py
+++ b/solution.py
@@ -139,7 +139,7 @@
 
 
 @functools.lru_cache(maxsize=None)
-def transform_tables(rows_total, ctx_count):
+def transform_tables(rows_total, ctx_count, least_bytes):
     length = rows_total * lanes
     bit_count = ctx_count.bit_length() - 1
     rev = np.array([int(format(j, "b").zfill(bit_count)[::-1], 2) if bit_count else 0 for j in range(ctx_count)])
@@ -158,7 +158,12 @@
     b1 = f1.conj().T / length
     v1 = np.concatenate([b1.real, -b1.imag], axis=1)
     half = lambda t: np.asarray(t, dtype=jnp.bfloat16)
-    return half(w1), half(w2), half(w3), half(v1), np.stack([tw.real, tw.imag]).astype(np.float32)
+    pieces = [w1.reshape(2 * rows_total, rows_total), v1[:, :rows_total], v1[:, rows_total:]]
+    square = np.concatenate([w2, w3], axis=1)
+    pieces.append(np.pad(square, ((0, 0), (0, max(rows_total - square.shape[1], 0)))))
+    turns = np.stack([tw.real, tw.imag]).astype(np.float32)
+    spare = np.zeros((2 * (least_bytes // turns.nbytes),) + turns.shape[1:], np.float32)
+    return np.concatenate(pieces).astype(jnp.bfloat16), np.concatenate([turns, spare])
 
 
 def greet_all(ctx_count, chan_count, me):
@@ -177,12 +182,11 @@
     return jnp.dot(a, b, preferred_element_type=jnp.float32)
 
 
-def fused_kernel(ctx_count, chan_count, skip_ref, v_hbm, k_hbm, gate_hbm, s_hbm, *refs):
-    tables_hbm, (out_ref,), tables = refs[:5], refs[5:6], refs[6:11]
-    w1_ref, w2_ref, w3_ref, v1_ref, tw_ref = tables
-    s_ref, stage, r_ref, x_ref, y_ref, g_ref = refs[11:17]
-    v_ref, k_ref, gate_ref, c_ref, o_ref = refs[17:22]
-    send_c, recv_c, send_s, recv_s, send_y, recv_y, local = refs[22:]
+def fused_kernel(ctx_count, chan_count, skip_hbm, v_hbm, k_hbm, gate_hbm, s_hbm, table_hbm, tw_hbm, out_ref, *refs):
+    skip_ref, w1_ref, w2_ref, w3_ref, v1_ref, tw_ref = refs[:6]
+    s_ref, stage, r_ref, x_ref, y_ref, g_ref, b_ref = refs[6:13]
+    v_ref, k_ref, gate_ref, c_ref, o_ref = refs[13:18]
+    sent, got_c, got_s, got_y, local = refs[18:]
     ctx, chan = lax.axis_index("ctx"), lax.axis_index("chan")
     me = ctx * chan_count + chan
     total = ctx_count * chan_count
@@ -190,18 +194,31 @@
     rows_total = x_ref.shape[1]
     block = stage.shape[2]
     local_channels = stage.shape[1]
-
+    wide = 2 * lanes
+
+    def load(index, source, target):
+        return pltpu.make_async_copy(source, target, local.at[index])
+
+    first_rows = 2 * rows_total
+    loads = [
+        load(0, v_hbm, v_ref),
+        load(1, k_hbm, k_ref),
+        load(2, s_hbm, s_ref),
+        load(3, table_hbm.at[pl.ds(0, first_rows)], w1_ref),
+        load(4, table_hbm.at[pl.ds(2 * first_rows, wide), pl.ds(0, wide)], w2_ref),
+        load(5, table_hbm.at[pl.ds(2 * first_rows, wide), pl.ds(wide, wide)], w3_ref),
+        load(6, tw_hbm.at[pl.ds(0, 2)], tw_ref),
+        load(7, table_hbm.at[pl.ds(first_rows, rows_total)], v1_ref.at[:, pl.ds(0, rows_total)]),
+        load(8, table_hbm.at[pl.ds(first_rows + rows_total, rows_total)], v1_ref.at[:, pl.ds(rows_total, rows_total)]),
+        load(9, gate_hbm, gate_ref),
+        load(10, skip_hbm, skip_ref),
+    ]
+    loads[0].start()
+    loads[1].start()
     greet_all(ctx_count, chan_count, me)
-    sources = (v_hbm, k_hbm, s_hbm, gate_hbm, *tables_hbm)
-    targets = (v_ref, k_ref, s_ref, gate_ref, *tables)
-    loads = [
-        pltpu.make_async_copy(source, target, local.at[i]) for i, (source, target) in enumerate(zip(sources, targets))
-    ]
-    for load in loads:
-        load.start()
+    for copy in loads[2:]:
+        copy.start()
     group = 2 * ctx_count
-    loads[0].wait()
-    loads[1].wait()
 
     def pack(pair):
         @pl.loop(0, chan_count)
@@ -213,7 +230,6 @@
             packed = jnp.concatenate([split[:, 0], split[:, 1]], axis=2)
             c_ref[pl.ds(index * ctx_count, ctx_count)] = packed.astype(jnp.bfloat16)
 
-
     def place(offset):
         other = lax.rem(me + offset, total)
         return other, other // chan_count, lax.rem(other, chan_count)
@@ -229,38 +245,39 @@
         return pltpu.make_async_remote_copy(
             src_ref=c_ref.at[slot(other_ctx, other_chan, pair)],
             dst_ref=x_ref.at[pair, my_rows],
-            send_sem=send_c.at[pair, offset - 1],
-            recv_sem=recv_c.at[pair, offset - 1],
+            send_sem=sent.at[0],
+            recv_sem=got_c.at[pair],
             device_id=(other_ctx, other_chan),
             device_id_type=MESH,
         )
 
-    def spectra_copy(pair, offset):
+    def spectra_copy(pair, first, count, offset):
         other_ctx = lax.rem(ctx + offset, ctx_count)
         return pltpu.make_async_remote_copy(
-            src_ref=stage.at[:, pl.ds((pair * ctx_count + other_ctx) * 2, 2)],
-            dst_ref=r_ref.at[:, pl.ds(2 * pair, 2), my_block],
-            send_sem=send_s.at[pair, offset - 1],
-            recv_sem=recv_s.at[pair, offset - 1],
+            src_ref=stage.at[:, pl.ds((pair * ctx_count + other_ctx) * 2 + first, count)],
+            dst_ref=r_ref.at[:, pl.ds(2 * pair + first, count), my_block],
+            send_sem=sent.at[1],
+            recv_sem=got_s.at[2 * pair + first],
             device_id=(other_ctx, chan),
             device_id_type=MESH,
         )
 
-    def result_copy(pair, offset):
-        other, other_ctx, other_chan = place(offset)
+    def columns(first, count):
+        return pl.ds(first * lanes, count * lanes)
+
+    def result_copy(pair, first, count, other):
+        other_ctx, other_chan = other // chan_count, lax.rem(other, chan_count)
         return pltpu.make_async_remote_copy(
-            src_ref=y_ref.at[pair, pl.ds(pl.multiple_of(other * rows, rows), rows)],
-            dst_ref=o_ref.at[slot(ctx, chan, pair)],
-            send_sem=send_y.at[pair, offset - 1],
-            recv_sem=recv_y.at[pair, offset - 1],
+            src_ref=y_ref.at[pair, pl.ds(pl.multiple_of(other * rows, rows), rows), columns(first, count)],
+            dst_ref=o_ref.at[slot(ctx, chan, pair), :, columns(first, count)],
+            send_sem=sent.at[2],
+            recv_sem=got_y.at[pair],
             device_id=(other_ctx, other_chan),
             device_id_type=MESH,
         )
 
-    def each(copy_of, pair, count, act):
-        @pl.loop(1, count)
-        def _(offset):
-            act(copy_of(pair, offset))
+    def settle(ref, sem):
+        pltpu.make_async_copy(ref, ref, sem).wait()
 
     def turned(part, channel):
         flipped = s_ref[part * local_channels + channel].T
@@ -275,35 +292,33 @@
                 for which in range(2):
                     stage[part, first + which] = turned(part, first + which)
 
+    def turn_own(pair):
         for part in range(2):
             for which in range(2):
                 r_ref[part, 2 * pair + which, my_block] = turned(part, (pair * ctx_count + ctx) * 2 + which)
         x_ref[pair, my_rows] = c_ref[slot(ctx, chan, pair)]
 
-    start = lambda copy: copy.start()
-    pack(0)
-    pl.semaphore_wait(pltpu.get_barrier_semaphore(), total - 1)
-    each(carried_copy, 0, total, start)
-    for pair in range(1, pairs):
-        pack(pair)
-        each(carried_copy, pair, total, start)
-    loads[2].wait()
-    for pair in range(pairs):
-        turn(pair)
-        each(spectra_copy, pair, ctx_count, start)
-    for load in loads[3:]:
-        load.wait()
+    def send_carried(pair):
+        @pl.loop(1, total)
+        def _(offset):
+            carried_copy(pair, offset).start()
+
+    def send_spectra(pair, first, count):
+        @pl.loop(1, ctx_count)
+        def _(offset):
+            spectra_copy(pair, first, count, offset).start()
+
     chunk = 2 * lanes
-    for pair in range(pairs):
-        each(carried_copy, pair, total, lambda copy: copy.wait_recv())
-        each(spectra_copy, pair, ctx_count, lambda copy: copy.wait_recv())
+
+    def forward(pair):
+        settle(c_ref.at[pl.ds(0, total - 1)], got_c.at[pair])
         x = x_ref.at[pair]
 
         @pl.loop(0, rows_total // chunk)
         def _(step):
             at = pl.ds(pl.multiple_of(step * chunk, chunk), chunk)
             below = pl.ds(pl.multiple_of(rows_total + step * chunk, chunk), chunk)
-            real, imag = dot(w1_ref[0, at], x[...]), dot(w1_ref[1, at], x[...])
+            real, imag = dot(w1_ref[at], x[...]), dot(w1_ref[below], x[...])
             t_real, t_imag = tw_ref[0, at], tw_ref[1, at]
             for which in range(2):
                 cols = slice(which * lanes, (which + 1) * lanes)
@@ -311,7 +326,19 @@
                 twiddled = jnp.concatenate(
                     [a_real * t_real - a_imag * t_imag, a_real * t_imag + a_imag * t_real], axis=1
                 )
-                bins = dot(twiddled.astype(jnp.bfloat16), w2_ref[...])
+                b_ref[2 * pair + which, at] = dot(twiddled.astype(jnp.bfloat16), w2_ref[...])
+
+    def backward(pair, first, count):
+        settle(stage.at[:, pl.ds(0, count * (ctx_count - 1))], got_s.at[2 * pair + first])
+
+        @pl.loop(0, rows_total // chunk)
+        def _(step):
+            at = pl.ds(pl.multiple_of(step * chunk, chunk), chunk)
+            below = pl.ds(pl.multiple_of(rows_total + step * chunk, chunk), chunk)
+            t_real, t_imag = tw_ref[0, at], tw_ref[1, at]
+            for which in range(first, first + count):
+                cols = slice(which * lanes, (which + 1) * lanes)
+                bins = b_ref[2 * pair + which, at]
                 b_real, b_imag = bins[:, :lanes], bins[:, lanes:]
                 f_real = r_ref[0, 2 * pair + which, at].astype(jnp.float32)
                 f_imag = r_ref[1, 2 * pair + which, at].astype(jnp.float32)
@@ -323,16 +350,29 @@
                 g_ref[at, cols] = (z_real * t_real + z_imag * t_imag).astype(jnp.bfloat16)
                 g_ref[below, cols] = (z_imag * t_real - z_real * t_imag).astype(jnp.bfloat16)
 
-        @pl.loop(0, rows_total // chunk)
+        steps = rows_total // chunk
+        spread = total // steps
+        home = me // spread
+        cols = slice(first * lanes, (first + count) * lanes)
+
+        @pl.loop(0, steps)
         def _(step):
-            at = pl.ds(pl.multiple_of(step * chunk, chunk), chunk)
-            y_ref[pair, at] = dot(v1_ref[at], g_ref[...]).astype(jnp.bfloat16)
-
-        o_ref[slot(ctx, chan, pair)] = y_ref[pair, my_rows]
-        each(result_copy, pair, total, start)
-
-    for pair in range(pairs):
-        each(result_copy, pair, total, lambda copy: copy.wait_recv())
+            turn_of = lax.rem(home + 1 + step, steps)
+            at = pl.ds(pl.multiple_of(turn_of * chunk, chunk), chunk)
+            y_ref[pair, at, cols] = dot(v1_ref[at], g_ref[:, cols]).astype(jnp.bfloat16)
+
+            @pl.loop(0, spread)
+            def _(index):
+                other = turn_of * spread + lax.rem(me + 1 + index, spread)
+
+                @pl.when(other != me)
+                def _():
+                    result_copy(pair, first, count, other).start()
+
+        o_ref[slot(ctx, chan, pair), :, cols] = y_ref[pair, my_rows, cols]
+
+    def finish(pair):
+        settle(o_ref.at[pl.ds(0, total - 1)], got_y.at[pair])
 
         @pl.loop(0, chan_count)
         def _(chan_index):
@@ -348,10 +388,63 @@
             at = pl.ds(pl.multiple_of(first * 2, group), group)
             out_ref[at] = (gate_ref[at].astype(jnp.float32) * flat).astype(jnp.bfloat16)
 
-    for pair in range(pairs):
-        each(carried_copy, pair, total, lambda copy: copy.wait_send())
-        each(spectra_copy, pair, ctx_count, lambda copy: copy.wait_send())
-        each(result_copy, pair, total, lambda copy: copy.wait_send())
+    waited = set()
+
+    def need(*indices):
+        for index in indices:
+            if index not in waited:
+                waited.add(index)
+                loads[index].wait()
+
+    need(0, 1)
+    pack(0)
+    need(0, 1)
+    pack(1)
+    need(0, 1)
+    pack(2)
+    pl.semaphore_wait(pltpu.get_barrier_semaphore(), total - 1)
+    send_carried(0)
+    send_carried(1)
+    send_carried(2)
+    need(2)
+    turn(0)
+    send_spectra(0, 0, 2)
+    need(2)
+    turn_own(0)
+    need(2)
+    turn(1)
+    send_spectra(1, 0, 2)
+    need(2)
+    turn_own(1)
+    need(2)
+    turn(2)
+    send_spectra(2, 0, 1)
+    send_spectra(2, 1, 1)
+    need(2)
+    turn_own(2)
+    need(3, 4, 6)
+    forward(0)
+    need(3, 4, 6)
+    forward(1)
+    need(5, 7, 8)
+    backward(0, 0, 2)
+    need(3, 4, 6)
+    forward(2)
+    need(5, 7, 8)
+    backward(1, 0, 2)
+    need(5, 7, 8)
+    backward(2, 0, 1)
+    need(5, 7, 8)
+    backward(2, 1, 1)
+    need(9, 10)
+    finish(0)
+    need(9, 10)
+    finish(1)
+    need(9, 10)
+    finish(2)
+    settle(c_ref.at[pl.ds(0, pairs * (total - 1))], sent.at[0])
+    settle(stage.at[:, pl.ds(0, 2 * pairs * (ctx_count - 1))], sent.at[1])
+    settle(o_ref.at[pl.ds(0, pairs * (total - 1))], sent.at[2])
 
 
 def channel_body(value_branch, key_branch, gate_branch, skip_gain, spectra):
@@ -363,36 +456,43 @@
     pairs = channels // total // 2
     local_channels = spectra.shape[1]
     block = spectra.shape[3] // lanes
-    tables = [jnp.asarray(t) for t in transform_tables(rows_total, ctx_count)]
+    table, turns = [jnp.asarray(t) for t in transform_tables(rows_total, ctx_count, 2 * channels * tokens)]
     sems = lambda *shape: pltpu.SemaphoreType.DMA(shape)
     hbm = pl.BlockSpec(memory_space=pl.ANY)
     packed = pltpu.VMEM((channels // 2, rows, 2 * lanes), jnp.bfloat16)
     held = pltpu.VMEM((channels, tokens), jnp.bfloat16)
+    half = lambda *shape: pltpu.VMEM(shape, jnp.bfloat16)
     return pl.pallas_call(
         functools.partial(fused_kernel, ctx_count, chan_count),
-        in_specs=[pl.BlockSpec(memory_space=pltpu.SMEM)] + [hbm] * 9,
+        in_specs=[hbm] * 7,
         out_specs=VMEM,
         out_shape=jax.ShapeDtypeStruct((channels, tokens), jnp.bfloat16),
-        scratch_shapes=[pltpu.VMEM(t.shape, t.dtype) for t in tables]
-        + [
+        scratch_shapes=[
+            pltpu.SMEM((channels,), jnp.float32),
+            half(2 * rows_total, rows_total),
+            half(2 * lanes, 2 * lanes),
+            half(2 * lanes, 2 * lanes),
+            half(rows_total, 2 * rows_total),
+            pltpu.VMEM((2, rows_total, lanes), jnp.float32),
             pltpu.VMEM((2 * local_channels, block, lanes), jnp.float32),
-            pltpu.VMEM((2, local_channels, block, lanes), jnp.bfloat16),
-            pltpu.VMEM((2, 2 * pairs, rows_total, lanes), jnp.bfloat16),
-            pltpu.VMEM((pairs, rows_total, 2 * lanes), jnp.bfloat16),
-            pltpu.VMEM((pairs, rows_total, 2 * lanes), jnp.bfloat16),
-            pltpu.VMEM((2 * rows_total, 2 * lanes), jnp.bfloat16),
+            half(2, local_channels, block, lanes),
+            half(2, 2 * pairs, rows_total, lanes),
+            half(pairs, rows_total, 2 * lanes),
+            half(pairs, rows_total, 2 * lanes),
+            half(2 * rows_total, 2 * lanes),
+            pltpu.VMEM((2 * pairs, rows_total, 2 * lanes), jnp.float32),
             held, held, held, packed, packed,
-        ]
-        + [sems(pairs, count - 1) for count in (total, total, ctx_count, ctx_count, total, total)]
-        + [sems(9)],
-        compiler_params=pltpu.CompilerParams(collective_id=0, has_side_effects=True),
+            sems(3), sems(pairs), sems(2 * pairs), sems(pairs), sems(11),
+        ],
+        compiler_params=pltpu.CompilerParams(collective_id=0, has_side_effects=True, vmem_limit_bytes=55369728),
     )(
         skip_gain,
         value_branch,
         key_branch,
         gate_branch,
         spectra.reshape(2 * local_channels, block, lanes),
-        *tables,
+        table,
+        turns,
     )
 
 

time: 56 us -> 46.6 us (0.83)
  Pallas kernels: 53.8 us -> 44.9 us
    pallas_call x1, Pallas kernels: 53.8 us -> 44.9 us  [channel_body(): pl.pallas_call(functools.partial(fused_kernel, ctx_count, chan_count), in...]
    unnamed x1 -> x3, local copies, waits for them, and re-layouts: 2.09 us -> 1.56 us
where the time goes in v1:
time: 46.6 us; the launch traced here: 46.5 us
  Pallas kernels  44.9 us (96%)
  local copies, waits for them, and re-layouts  1.56 us (3%)
    pallas_call x1, Pallas kernels, channel_body(): pl.pallas_call(functools.partial(fused_kernel, ctx_count, chan_count), in...  44.9 us
    unnamed x3, local copies, waits for them, and re-layouts  1.56 us

profile of v1, /device:TPU:0, one launch (start us, length us, event | category | flops | bytes accessed | tf_op | source)
XLA Modules:
  0.0 46.5 jit_solution(9225232192842927670)
XLA Ops:
  0.0 0.0 copy-start
  0.0 0.7 %copy-done = f32[192]{0:T(256)S(1)} copy-done((f32[192]{0:T(256)S(1)}, f32[192]{0:T(256)}, u32[]{:S(2)}) %copy-start) | copy-done | bytes 792
  0.7 44.9 %shard_map.73 = bf16[192,2048]{1,0:T(8,128)(2,1)S(1)} custom-call(f32[192]{0:T(256)S(1)} %copy-done, bf16[192,2048]{1,0:T(8,128)(2,1)} %v_hbm.1, bf16[192,2048]{1,0:T(8,128)(2,1)} %k_hbm.1, bf16[192,2048]{1,0:T(8,128)(2,1)} %gate_hbm.1, f32[96,64,128]{2,1,0:T(8,128)} %bitcast.1, bf16[2304,512]{1,0:T(8,128)(2,1)} %constant.4.clone.table_hbm, ...), custom_call_target="tpu_custom_call" | custom-call | tf_op jit(solution)/shard_map/pallas_call | solution.py:465
  45.6 0.9 %copy.9 = bf16[192,2048]{1,0:T(8,128)(2,1)} copy(bf16[192,2048]{1,0:T(8,128)(2,1)S(1)} %shard_map.73) | data formatting | bytes 1572864
Async XLA Ops:
  0.0 0.7 %copy-start = (f32[192]{0:T(256)S(1)}, f32[192]{0:T(256)}, u32[]{:S(2)}) copy-start(f32[192]{0:T(256)} %skip_hbm.1) | copy-start | bytes 2308

commit v2 on v1

--- a/solution.py
+++ b/solution.py
@@ -166,18 +166,6 @@
     return np.concatenate(pieces).astype(jnp.bfloat16), np.concatenate([turns, spare])
 
 
-def greet_all(ctx_count, chan_count, me):
-    total = ctx_count * chan_count
-    barrier = pltpu.get_barrier_semaphore()
-
-    @pl.loop(1, total)
-    def _(offset):
-        other = lax.rem(me + offset, total)
-        pl.semaphore_signal(
-            barrier, inc=1, device_id=(other // chan_count, lax.rem(other, chan_count)), device_id_type=MESH
-        )
-
-
 def dot(a, b):
     return jnp.dot(a, b, preferred_element_type=jnp.float32)
 
@@ -186,7 +174,7 @@
     skip_ref, w1_ref, w2_ref, w3_ref, v1_ref, tw_ref = refs[:6]
     s_ref, stage, r_ref, x_ref, y_ref, g_ref, b_ref = refs[6:13]
     v_ref, k_ref, gate_ref, c_ref, o_ref = refs[13:18]
-    sent, got_c, got_s, got_y, local = refs[18:]
+    sent, got_c, got_s, got_y, local, ready = refs[18:]
     ctx, chan = lax.axis_index("ctx"), lax.axis_index("chan")
     me = ctx * chan_count + chan
     total = ctx_count * chan_count
@@ -200,10 +188,12 @@
         return pltpu.make_async_copy(source, target, local.at[index])
 
     first_rows = 2 * rows_total
+    share = 2 * ctx_count
+    rest = local_channels - share
     loads = [
         load(0, v_hbm, v_ref),
         load(1, k_hbm, k_ref),
-        load(2, s_hbm, s_ref),
+        load(2, s_hbm.at[pl.ds(0, share)], s_ref.at[pl.ds(0, share)]),
         load(3, table_hbm.at[pl.ds(0, first_rows)], w1_ref),
         load(4, table_hbm.at[pl.ds(2 * first_rows, wide), pl.ds(0, wide)], w2_ref),
         load(5, table_hbm.at[pl.ds(2 * first_rows, wide), pl.ds(wide, wide)], w3_ref),
@@ -212,12 +202,32 @@
         load(8, table_hbm.at[pl.ds(first_rows + rows_total, rows_total)], v1_ref.at[:, pl.ds(rows_total, rows_total)]),
         load(9, gate_hbm, gate_ref),
         load(10, skip_hbm, skip_ref),
+        load(11, s_hbm.at[pl.ds(local_channels, share)], s_ref.at[pl.ds(local_channels, share)]),
+        load(12, s_hbm.at[pl.ds(share, rest)], s_ref.at[pl.ds(share, rest)]),
+        load(13, s_hbm.at[pl.ds(local_channels + share, rest)], s_ref.at[pl.ds(local_channels + share, rest)]),
     ]
-    loads[0].start()
-    loads[1].start()
-    greet_all(ctx_count, chan_count, me)
-    for copy in loads[2:]:
-        copy.start()
+    barrier = pltpu.get_barrier_semaphore()
+    even = lax.rem(ctx, 2) == 0
+    partner = (ctx + 1 - 2 * lax.rem(ctx, 2), chan)
+
+    def signal(semaphore, device):
+        pl.semaphore_signal(semaphore, inc=1, device_id=device, device_id_type=MESH)
+
+    for index in (0, 1, 2, 11):
+        loads[index].start()
+
+    @pl.loop(0, ctx_count // 2)
+    def _(chip):
+        @pl.when(2 * chip != ctx)
+        def _():
+            signal(barrier, (2 * chip, chan))
+
+        @pl.loop(1, chan_count)
+        def _(offset):
+            signal(barrier, (2 * chip + 1, lax.rem(chan + offset, chan_count)))
+
+    for index in (12, 13, 3, 4, 6, 5, 7, 8, 9, 10):
+        loads[index].start()
     group = 2 * ctx_count
 
     def pack(pair):
@@ -280,16 +290,16 @@
         pltpu.make_async_copy(ref, ref, sem).wait()
 
     def turned(part, channel):
-        flipped = s_ref[part * local_channels + channel].T
+        flipped = s_ref[part * local_channels + channel].astype(jnp.bfloat16).T
         pieces = [flipped[f * block : (f + 1) * block] for f in range(flipped.shape[0] // block)]
         return jnp.concatenate(pieces, axis=1).astype(jnp.bfloat16)
 
-    def turn(pair):
+    def turn(pair, begin, count):
         @pl.loop(1, ctx_count)
         def _(offset):
             first = (pair * ctx_count + lax.rem(ctx + offset, ctx_count)) * 2
             for part in range(2):
-                for which in range(2):
+                for which in range(begin, begin + count):
                     stage[part, first + which] = turned(part, first + which)
 
     def turn_own(pair):
@@ -388,6 +398,26 @@
             at = pl.ds(pl.multiple_of(first * 2, group), group)
             out_ref[at] = (gate_ref[at].astype(jnp.float32) * flat).astype(jnp.bfloat16)
 
+    def meet_plane():
+        @pl.when(even)
+        def _():
+            pl.semaphore_wait(barrier, ctx_count - 1)
+            signal(ready, partner)
+
+        @pl.when(jnp.logical_not(even))
+        def _():
+            pl.semaphore_wait(ready, 1)
+
+    def meet_all():
+        @pl.when(jnp.logical_not(even))
+        def _():
+            pl.semaphore_wait(barrier, ctx_count * (chan_count - 1))
+            signal(ready, partner)
+
+        @pl.when(even)
+        def _():
+            pl.semaphore_wait(ready, 1)
+
     waited = set()
 
     def need(*indices):
@@ -402,36 +432,42 @@
     pack(1)
     need(0, 1)
     pack(2)
-    pl.semaphore_wait(pltpu.get_barrier_semaphore(), total - 1)
+    meet_plane()
+    meet_all()
     send_carried(0)
     send_carried(1)
     send_carried(2)
-    need(2)
-    turn(0)
-    send_spectra(0, 0, 2)
-    need(2)
-    turn_own(0)
-    need(2)
-    turn(1)
+    need(2, 11)
+    turn(0, 0, 1)
+    send_spectra(0, 0, 1)
+    need(2, 11)
+    turn(0, 1, 1)
+    send_spectra(0, 1, 1)
+    need(12, 13)
+    turn(1, 0, 2)
     send_spectra(1, 0, 2)
-    need(2)
-    turn_own(1)
-    need(2)
-    turn(2)
+    need(12, 13)
+    turn(2, 0, 2)
     send_spectra(2, 0, 1)
     send_spectra(2, 1, 1)
-    need(2)
+    need(2, 11)
+    turn_own(0)
+    need(12, 13)
+    turn_own(1)
+    need(12, 13)
     turn_own(2)
     need(3, 4, 6)
     forward(0)
+    need(5, 7, 8)
+    backward(0, 0, 1)
     need(3, 4, 6)
     forward(1)
     need(5, 7, 8)
-    backward(0, 0, 2)
+    backward(0, 1, 1)
+    need(5, 7, 8)
+    backward(1, 0, 2)
     need(3, 4, 6)
     forward(2)
-    need(5, 7, 8)
-    backward(1, 0, 2)
     need(5, 7, 8)
     backward(2, 0, 1)
     need(5, 7, 8)
@@ -482,11 +518,11 @@
             half(2 * rows_total, 2 * lanes),
             pltpu.VMEM((2 * pairs, rows_total, 2 * lanes), jnp.float32),
             held, held, held, packed, packed,
-            sems(3), sems(pairs), sems(2 * pairs), sems(pairs), sems(11),
+            sems(3), sems(pairs), sems(2 * pairs), sems(pairs), sems(14), pltpu.SemaphoreType.REGULAR,
         ],
         compiler_params=pltpu.CompilerParams(collective_id=0, has_side_effects=True, vmem_limit_bytes=55369728),
     )(
-        skip_gain,
+        pltpu.with_memory_space_constraint(skip_gain, pltpu.HBM),
         value_branch,
         key_branch,
         gate_branch,

time: 46.6 us -> 45.3 us (0.972)
  local copies, waits for them, and re-layouts: 1.56 us -> 0.88 us
  Pallas kernels: 44.9 us -> 44.3 us
    unnamed x3 -> x1, local copies, waits for them, and re-layouts: 1.56 us -> 0.88 us
    pallas_call x1, Pallas kernels: 44.9 us -> 44.3 us  [channel_body(): pl.pallas_call(functools.partial(fused_kernel, ctx_count, chan_count), in...]
where the time goes in v2:
time: 45.3 us; the launch traced here: 45.2 us
  Pallas kernels  44.3 us (98%)
  local copies, waits for them, and re-layouts  0.88 us (2%)
    pallas_call x1, Pallas kernels, channel_body(): pl.pallas_call(functools.partial(fused_kernel, ctx_count, chan_count), in...  44.3 us

profile of v2, /device:TPU:0, one launch (start us, length us, event | category | flops | bytes accessed | tf_op | source)
XLA Modules:
  0.0 45.2 jit_solution(6012469889211299420)
XLA Ops:
  0.0 44.3 %shard_map.73 = bf16[192,2048]{1,0:T(8,128)(2,1)S(1)} custom-call(f32[192]{0:T(256)} %skip_hbm.1, bf16[192,2048]{1,0:T(8,128)(2,1)} %v_hbm.1, bf16[192,2048]{1,0:T(8,128)(2,1)} %k_hbm.1, bf16[192,2048]{1,0:T(8,128)(2,1)} %gate_hbm.1, f32[96,64,128]{2,1,0:T(8,128)} %bitcast.1, bf16[2304,512]{1,0:T(8,128)(2,1)} %constant.4.clone.table_hbm, ...), custom_call_target="tpu_custom_call" | custom-call | tf_op jit(solution)/shard_map/pallas_call | solution.py:501
  44.3 0.9 %copy.9 = bf16[192,2048]{1,0:T(8,128)(2,1)} copy(bf16[192,2048]{1,0:T(8,128)(2,1)S(1)} %shard_map.73) | data formatting | bytes 1572864

commit v3 on v2

--- a/solution.py
+++ b/solution.py
@@ -166,6 +166,14 @@
     return np.concatenate(pieces).astype(jnp.bfloat16), np.concatenate([turns, spare])
 
 
+def wrap(number, count):
+    return number & (count - 1) if count & (count - 1) == 0 else lax.rem(number, count)
+
+
+def over(number, count):
+    return number >> (count.bit_length() - 1) if count & (count - 1) == 0 else number // count
+
+
 def dot(a, b):
     return jnp.dot(a, b, preferred_element_type=jnp.float32)
 
@@ -241,8 +249,8 @@
             c_ref[pl.ds(index * ctx_count, ctx_count)] = packed.astype(jnp.bfloat16)
 
     def place(offset):
-        other = lax.rem(me + offset, total)
-        return other, other // chan_count, lax.rem(other, chan_count)
+        other = wrap(me + offset, total)
+        return other, over(other, chan_count), wrap(other, chan_count)
 
     def slot(ctx_index, chan_index, pair):
         return (chan_index * pairs + pair) * ctx_count + ctx_index
@@ -262,7 +270,7 @@
         )
 
     def spectra_copy(pair, first, count, offset):
-        other_ctx = lax.rem(ctx + offset, ctx_count)
+        other_ctx = wrap(ctx + offset, ctx_count)
         return pltpu.make_async_remote_copy(
             src_ref=stage.at[:, pl.ds((pair * ctx_count + other_ctx) * 2 + first, count)],
             dst_ref=r_ref.at[:, pl.ds(2 * pair + first, count), my_block],
@@ -276,12 +284,12 @@
         return pl.ds(first * lanes, count * lanes)
 
     def result_copy(pair, first, count, other):
-        other_ctx, other_chan = other // chan_count, lax.rem(other, chan_count)
+        other_ctx, other_chan = over(other, chan_count), wrap(other, chan_count)
         return pltpu.make_async_remote_copy(
             src_ref=y_ref.at[pair, pl.ds(pl.multiple_of(other * rows, rows), rows), columns(first, count)],
             dst_ref=o_ref.at[slot(ctx, chan, pair), :, columns(first, count)],
             send_sem=sent.at[2],
-            recv_sem=got_y.at[pair],
+            recv_sem=got_y.at[pair, chan],
             device_id=(other_ctx, other_chan),
             device_id_type=MESH,
         )
@@ -373,7 +381,7 @@
 
             @pl.loop(0, spread)
             def _(index):
-                other = turn_of * spread + lax.rem(me + 1 + index, spread)
+                other = turn_of * spread + wrap(me + 1 + index, spread)
 
                 @pl.when(other != me)
                 def _():
@@ -382,21 +390,27 @@
         o_ref[slot(ctx, chan, pair), :, cols] = y_ref[pair, my_rows, cols]
 
     def finish(pair):
-        settle(o_ref.at[pl.ds(0, total - 1)], got_y.at[pair])
-
-        @pl.loop(0, chan_count)
-        def _(chan_index):
-            first = slot(0, chan_index, pair)
-            sums = []
-            for i in range(ctx_count):
-                for which in range(2):
-                    cols = slice(which * lanes, (which + 1) * lanes)
-                    carried = c_ref[first + i, :, cols].astype(jnp.float32)
-                    gain = skip_ref[2 * (first + i) + which]
-                    sums.append(o_ref[first + i, :, cols].astype(jnp.float32) + gain * carried)
-            flat = jnp.stack(sums).reshape(group, rows * lanes)
-            at = pl.ds(pl.multiple_of(first * 2, group), group)
-            out_ref[at] = (gate_ref[at].astype(jnp.float32) * flat).astype(jnp.bfloat16)
+        settle(o_ref.at[pl.ds(0, ctx_count - 1)], got_y.at[pair, chan])
+        gate_group(pair, chan)
+
+        @pl.loop(1, chan_count)
+        def _(offset):
+            chan_index = lax.rem(chan + offset, chan_count)
+            settle(o_ref.at[pl.ds(0, ctx_count)], got_y.at[pair, chan_index])
+            gate_group(pair, chan_index)
+
+    def gate_group(pair, chan_index):
+        first = slot(0, chan_index, pair)
+        sums = []
+        for i in range(ctx_count):
+            for which in range(2):
+                cols = slice(which * lanes, (which + 1) * lanes)
+                carried = c_ref[first + i, :, cols].astype(jnp.float32)
+                gain = skip_ref[2 * (first + i) + which]
+                sums.append(o_ref[first + i, :, cols].astype(jnp.float32) + gain * carried)
+        flat = jnp.stack(sums).reshape(group, rows * lanes)
+        at = pl.ds(pl.multiple_of(first * 2, group), group)
+        out_ref[at] = (gate_ref[at].astype(jnp.float32) * flat).astype(jnp.bfloat16)
 
     def meet_plane():
         @pl.when(even)
@@ -444,30 +458,35 @@
     turn(0, 1, 1)
     send_spectra(0, 1, 1)
     need(12, 13)
-    turn(1, 0, 2)
-    send_spectra(1, 0, 2)
+    turn(1, 0, 1)
+    send_spectra(1, 0, 1)
+    need(12, 13)
+    turn(1, 1, 1)
+    send_spectra(1, 1, 1)
     need(12, 13)
     turn(2, 0, 2)
     send_spectra(2, 0, 1)
     send_spectra(2, 1, 1)
     need(2, 11)
     turn_own(0)
-    need(12, 13)
-    turn_own(1)
-    need(12, 13)
-    turn_own(2)
     need(3, 4, 6)
     forward(0)
     need(5, 7, 8)
     backward(0, 0, 1)
+    need(12, 13)
+    turn_own(1)
     need(3, 4, 6)
     forward(1)
     need(5, 7, 8)
     backward(0, 1, 1)
     need(5, 7, 8)
-    backward(1, 0, 2)
+    backward(1, 0, 1)
+    need(12, 13)
+    turn_own(2)
     need(3, 4, 6)
     forward(2)
+    need(5, 7, 8)
+    backward(1, 1, 1)
     need(5, 7, 8)
     backward(2, 0, 1)
     need(5, 7, 8)
@@ -518,7 +537,7 @@
             half(2 * rows_total, 2 * lanes),
             pltpu.VMEM((2 * pairs, rows_total, 2 * lanes), jnp.float32),
             held, held, held, packed, packed,
-            sems(3), sems(pairs), sems(2 * pairs), sems(pairs), sems(14), pltpu.SemaphoreType.REGULAR,
+            sems(3), sems(pairs), sems(2 * pairs), sems(pairs, chan_count), sems(14), pltpu.SemaphoreType.REGULAR,
         ],
         compiler_params=pltpu.CompilerParams(collective_id=0, has_side_effects=True, vmem_limit_bytes=55369728),
     )(

time: 45.3 us -> 45.2 us (level)
  no operation moved by 1% of the time
where the time goes in v3:
time: 45.2 us; the launch traced here: 45.1 us
  Pallas kernels  44.2 us (98%)
  local copies, waits for them, and re-layouts  0.88 us (2%)
    pallas_call x1, Pallas kernels, channel_body(): pl.pallas_call(functools.partial(fused_kernel, ctx_count, chan_count), in...  44.2 us

profile of v3, /device:TPU:0, one launch (start us, length us, event | category | flops | bytes accessed | tf_op | source)
XLA Modules:
  0.0 45.1 jit_solution(15403320299038929692)
XLA Ops:
  0.0 44.2 %shard_map.73 = bf16[192,2048]{1,0:T(8,128)(2,1)S(1)} custom-call(f32[192]{0:T(256)} %skip_hbm.1, bf16[192,2048]{1,0:T(8,128)(2,1)} %v_hbm.1, bf16[192,2048]{1,0:T(8,128)(2,1)} %k_hbm.1, bf16[192,2048]{1,0:T(8,128)(2,1)} %gate_hbm.1, f32[96,64,128]{2,1,0:T(8,128)} %bitcast.1, bf16[2304,512]{1,0:T(8,128)(2,1)} %constant.4.clone.table_hbm, ...), custom_call_target="tpu_custom_call" | custom-call | tf_op jit(solution)/shard_map/pallas_call | solution.py:520
  44.2 0.9 %copy.9 = bf16[192,2048]{1,0:T(8,128)(2,1)} copy(bf16[192,2048]{1,0:T(8,128)(2,1)S(1)} %shard_map.73) | data formatting | bytes 1572864

commit v4 on v3

--- a/solution.py
+++ b/solution.py
@@ -368,7 +368,7 @@
                 g_ref[at, cols] = (z_real * t_real + z_imag * t_imag).astype(jnp.bfloat16)
                 g_ref[below, cols] = (z_imag * t_real - z_real * t_imag).astype(jnp.bfloat16)
 
-        steps = rows_total // chunk
+        steps = rows_total // lanes
         spread = total // steps
         home = me // spread
         cols = slice(first * lanes, (first + count) * lanes)
@@ -376,7 +376,7 @@
         @pl.loop(0, steps)
         def _(step):
             turn_of = lax.rem(home + 1 + step, steps)
-            at = pl.ds(pl.multiple_of(turn_of * chunk, chunk), chunk)
+            at = pl.ds(pl.multiple_of(turn_of * lanes, lanes), lanes)
             y_ref[pair, at, cols] = dot(v1_ref[at], g_ref[:, cols]).astype(jnp.bfloat16)
 
             @pl.loop(0, spread)

time: 45.2 us -> 45.1 us (level)
  no operation moved by 1% of the time
where the time goes in v4:
time: 45.1 us; the launch traced here: 45 us
  Pallas kernels  44.1 us (98%)
  local copies, waits for them, and re-layouts  0.88 us (2%)
    pallas_call x1, Pallas kernels, channel_body(): pl.pallas_call(functools.partial(fused_kernel, ctx_count, chan_count), in...  44.1 us

profile of v4, /device:TPU:0, one launch (start us, length us, event | category | flops | bytes accessed | tf_op | source)
XLA Modules:
  0.0 45.0 jit_solution(10083330712018315153)
XLA Ops:
  0.0 44.1 %shard_map.73 = bf16[192,2048]{1,0:T(8,128)(2,1)S(1)} custom-call(f32[192]{0:T(256)} %skip_hbm.1, bf16[192,2048]{1,0:T(8,128)(2,1)} %v_hbm.1, bf16[192,2048]{1,0:T(8,128)(2,1)} %k_hbm.1, bf16[192,2048]{1,0:T(8,128)(2,1)} %gate_hbm.1, f32[96,64,128]{2,1,0:T(8,128)} %bitcast.1, bf16[2304,512]{1,0:T(8,128)(2,1)} %constant.4.clone.table_hbm, ...), custom_call_target="tpu_custom_call" | custom-call | tf_op jit(solution)/shard_map/pallas_call | solution.py:520
  44.1 0.9 %copy.9 = bf16[192,2048]{1,0:T(8,128)(2,1)} copy(bf16[192,2048]{1,0:T(8,128)(2,1)S(1)} %shard_map.73) | data formatting | bytes 1572864

commit v5 on v4

--- a/solution.py
+++ b/solution.py
@@ -442,14 +442,14 @@
 
     need(0, 1)
     pack(0)
-    need(0, 1)
-    pack(1)
-    need(0, 1)
-    pack(2)
     meet_plane()
     meet_all()
     send_carried(0)
+    need(0, 1)
+    pack(1)
     send_carried(1)
+    need(0, 1)
+    pack(2)
     send_carried(2)
     need(2, 11)
     turn(0, 0, 1)

time: 45.1 us -> 45.2 us (level)
  no operation moved by 1% of the time
where the time goes in v5:
time: 45.2 us; the launch traced here: 45.1 us
  Pallas kernels  44.2 us (98%)
  local copies, waits for them, and re-layouts  0.88 us (2%)
    pallas_call x1, Pallas kernels, channel_body(): pl.pallas_call(functools.partial(fused_kernel, ctx_count, chan_count), in...  44.2 us

profile of v5, /device:TPU:0, one launch (start us, length us, event | category | flops | bytes accessed | tf_op | source)
XLA Modules:
  0.0 45.1 jit_solution(5443401848906171184)
XLA Ops:
  0.0 44.2 %shard_map.73 = bf16[192,2048]{1,0:T(8,128)(2,1)S(1)} custom-call(f32[192]{0:T(256)} %skip_hbm.1, bf16[192,2048]{1,0:T(8,128)(2,1)} %v_hbm.1, bf16[192,2048]{1,0:T(8,128)(2,1)} %k_hbm.1, bf16[192,2048]{1,0:T(8,128)(2,1)} %gate_hbm.1, f32[96,64,128]{2,1,0:T(8,128)} %bitcast.1, bf16[2304,512]{1,0:T(8,128)(2,1)} %constant.4.clone.table_hbm, ...), custom_call_target="tpu_custom_call" | custom-call | tf_op jit(solution)/shard_map/pallas_call | solution.py:520
  44.2 0.9 %copy.9 = bf16[192,2048]{1,0:T(8,128)(2,1)} copy(bf16[192,2048]{1,0:T(8,128)(2,1)S(1)} %shard_map.73) | data formatting | bytes 1572864
